TPU v7x, 256 devices: a whole 4x4x8 slice. The times are simulated.
256 devices in a mesh: rows: 4 (over y), half: 2 (over core), obs: 32 (over z, x).
Axes of the slice: x: 4, y: 4, z: 8, core: 2. Of those that a mesh axis runs over, the one named last changes fastest.
Arguments:
- ens_state: bfloat16 [2, 8192, 256], P('half', ('rows', 'obs')), may hold values from -6 to 6
- state_pos: bfloat16 [8192], P(('rows', 'obs')), may hold values from 0 to 1
- obs_ens: bfloat16 [2, 2, 65536, 256], P(None, 'half', ('rows', 'obs')), may hold values from -6 to 6
- obs_pos: bfloat16 [2, 65536], P(None, ('rows', 'obs')), may hold values from 0 to 1
- innov_weight: bfloat16 [2, 2, 65536, 256], P(None, 'half', ('rows', 'obs')), may hold values from -0.875 to 0.875
- block_rows: int32 [2, 512, 16], replicated, may hold values from 0 to 63, as said below
Outputs:
- increment: float32 [2, 8192, 256], P('half', ('rows', 'obs'))
Inputs may be any that keep to these rules, and one draw needn't show every extreme that they name: `block_rows`: each row lists 16 different state blocks. Counting state blocks in aligned ranges of 16, an observation block names at most 8 blocks of one range, and in every aligned group of 16 observation blocks some range is named exactly 8 times by each block of the group.
All inputs are finite; a program needn't handle non-finite values.
Results may differ from a plain program's by a relative error of at most 0.0029.
Values may be sent and summed in bfloat16 or wider, within the bound.
No kernel may reach another device: no remote copies, remote signals or barrier semaphores. Data moves between devices by JAX's collectives and lax.ppermute only.
A program may use at most 64 MiB of HBM per device.

v0:
```python
import jax
import jax.numpy as jnp
from jax import lax
from jax.sharding import PartitionSpec as P

ROW_BLOCKS = 16
OBS_BLOCKS = 16
BATCHES = 2


def partner(value, axis, bit):
    mask = 2**bit
    pairs = [(source, source ^ mask) for source in range(lax.axis_size(axis))]
    return lax.ppermute(value, axis, pairs)


def slot_tables(picked, first_block, row_blocks):
    blocks_iota = jnp.arange(row_blocks, dtype=jnp.int32)
    relative = picked - first_block
    present = jnp.sum(
        (relative[:, :, None] == blocks_iota[None, None, :]).astype(jnp.int32), axis=1
    )
    ranking = jnp.cumsum(present, axis=1) - 1
    slot_iota = jnp.arange(row_blocks // 2, dtype=jnp.int32)
    chosen = present[:, :, None] * (ranking[:, :, None] == slot_iota[None, None, :]).astype(
        jnp.int32
    )
    slot_block = jnp.sum(chosen * blocks_iota[None, :, None], axis=1)
    slot_live = jnp.sum(chosen, axis=1)
    return (slot_block, slot_live)


def batch_increment(state_rows, row_places, obs_rows, obs_places, weights, picked, first_block):
    row_blocks = ROW_BLOCKS
    edge_size = obs_rows.shape[0] // picked.shape[0]
    member_count = state_rows.shape[1]
    state_tiles = state_rows.reshape(row_blocks, edge_size, member_count)
    place_tiles = row_places.astype(jnp.float32).reshape(row_blocks, edge_size)
    slot_block, slot_live = slot_tables(picked, first_block, row_blocks)

    def visit(running, entries):
        obs_tile, obs_place, weight_tile, blocks_here, live_here = entries
        gathered = state_tiles[blocks_here].reshape(-1, member_count)
        positions = place_tiles[blocks_here].reshape(-1)
        products = lax.dot_general(
            gathered, obs_tile, (((1,), (1,)), ((), ())), preferred_element_type=jnp.float32
        )
        distance = positions[:, None] - obs_place[None, :]
        damping = jnp.exp(-4.0 * distance * distance)
        live_rows = jnp.repeat(live_here.astype(jnp.float32), edge_size)
        scaled = (products * damping / (member_count - 1) * live_rows[:, None]).astype(jnp.bfloat16)
        additions = jnp.dot(scaled, weight_tile, preferred_element_type=jnp.float32)
        running = running.at[blocks_here].add(additions.reshape(-1, edge_size, member_count))
        return (running, None)

    initial = jnp.zeros((row_blocks, edge_size, member_count), jnp.float32)
    entries = (
        obs_rows.reshape(-1, edge_size, member_count),
        obs_places.astype(jnp.float32).reshape(-1, edge_size),
        weights.reshape(-1, edge_size, member_count),
        slot_block,
        slot_live,
    )
    running, _ = lax.scan(visit, initial, entries)
    return running.reshape(row_blocks * edge_size, member_count)


def local(ens_state, state_pos, obs_ens, obs_pos, innov_weight, block_rows):
    state_own, obs_own = (ens_state, obs_ens)
    weight_own = partner(innov_weight, "half", 0)
    place_column = obs_pos[:, None, :, None]
    obs_full, weight_full, place_full_obs = (
        lax.all_gather(obs_own, "rows", axis=2, tiled=True),
        lax.all_gather(weight_own, "rows", axis=2, tiled=True),
        lax.all_gather(place_column, "rows", axis=2, tiled=True),
    )
    state_full, place_full = (
        lax.all_gather(state_own[0], "obs", axis=0, tiled=True),
        lax.all_gather(state_pos, "obs", axis=0, tiled=True),
    )
    first_block = lax.axis_index("rows") * ROW_BLOCKS
    obs_count = lax.axis_size("obs")
    row_count = lax.axis_size("rows")
    span_blocks = OBS_BLOCKS // row_count
    block_ids = (
        (jnp.arange(row_count, dtype=jnp.int32)[:, None] * obs_count + lax.axis_index("obs"))
        * span_blocks
        + jnp.arange(span_blocks, dtype=jnp.int32)[None, :]
    ).reshape(-1)
    shares = None
    summed = None
    for batch_index in range(BATCHES):
        picked_here = block_rows[batch_index][block_ids]
        partial_value = batch_increment(
            state_full,
            place_full,
            obs_full[batch_index, 0],
            place_full_obs[batch_index, 0, :, 0],
            weight_full[batch_index, 0],
            picked_here,
            first_block,
        )
        summed = partial_value if summed is None else summed + partial_value
    shares = lax.psum_scatter(summed, "obs", scatter_dimension=0, tiled=True)
    shares = partner(shares, "half", 0)
    return shares[None]


def solution(mesh):
    in_specs = (
        P("half", ("rows", "obs"), None),
        P(("rows", "obs")),
        P(None, "half", ("rows", "obs"), None),
        P(None, ("rows", "obs")),
        P(None, "half", ("rows", "obs"), None),
        P(),
    )
    out_specs = P("half", ("rows", "obs"), None)
    return jax.shard_map(local, mesh=mesh, in_specs=in_specs, out_specs=out_specs, check_vma=False)
```

profile of v0, /device:TPU:1, one launch (start us, length us, event | category | flops | bytes accessed | tf_op | source)
XLA Modules:
  0.0 588.6 jit_solution(8644609748980073932)
XLA Ops:
  7.3 3.3 collective-permute-start
  10.6 1.7 collective-permute-done
  18.8 62.3 %all-reduce = bf16[2048]{0:T(1024)(128)(2,1)S(1)} all-reduce(bf16[2048]{0:T(1024)(128)(2,1)S(1)} %dynamic-update-slice), channel_id=1, replica_groups=mesh['rows'=4,'half'=2,'obs'=32] {'obs'}, use_global_device_ids=true, to_apply=%add | all-reduce | flops 2048 | bytes 8192
  81.0 8.7 %all-gather.1 = bf16[2,2048]{1,0:T(2,128)(2,1)S(1)} all-gather(bf16[2,512]{1,0:T(2,128)(2,1)S(1)} %copy-done.2), channel_id=3, replica_groups=mesh['rows'=4,'half'=2,'obs'=32] {'rows'}, dimensions={1}, use_global_device_ids=true | all-gather | bytes 10240 | tf_op jit(solution)/shard_map/all_gather | solution.py:75
  90.7 3.0 fusion.36
  93.7 3.0 fusion.35
  96.7 58.7 %all-gather.10.cloned.1.call-done = bf16[1,2048,256]{2,1,0:T(8,128)(2,1)} async-done(((bf16[1,64,256]{2,1,0:T(8,128)(2,1)}), bf16[1,2048,256]{2,1,0:T(8,128)(2,1)}) %all-gather.10.cloned.1.call-update) | async-done | bytes 1048592 | tf_op jit(solution)/shard_map/all_gather | solution.py:78
  155.6 99.0 %while.21 = (s32[]{:T(128)}, f32[16,128,256]{2,1,0:T(8,128)S(1)}, s32[16,8]{1,0:T(8,128)S(1)}, bf16[16,128,256]{2,1,0:T(8,128)(2,1)}, bf16[16,128,256]{2,1,0:T(8...) while((s32[]{:T(128)}, f32[16,128,256]{2,1,0:T(8,128)S(1)}, ...), condition=%wide.region_13.14_spmd, body=%wide.region_11.13_spmd.sunk | while | flops 135267360 | bytes 6450065 | solution.py:64
  155.7 1.8 gather_fusion.2
  160.5 1.3 scatter_fusion.1
  161.9 1.8 gather_fusion.2
  166.7 1.3 scatter_fusion.1
  168.1 1.8 gather_fusion.2
  174.3 1.8 gather_fusion.2
  180.5 1.8 gather_fusion.2
  186.7 1.8 gather_fusion.2
  192.9 1.8 gather_fusion.2
  199.0 1.8 gather_fusion.2
  205.2 1.8 gather_fusion.2
  211.4 1.8 gather_fusion.2
  217.6 1.8 gather_fusion.2
  223.8 1.8 gather_fusion.2
  230.0 1.8 gather_fusion.2
  236.2 1.8 gather_fusion.2
  242.4 1.8 gather_fusion.2
  248.5 1.8 gather_fusion.2
  254.7 1.3 copy-done
  256.2 99.1 %while.20 = (s32[]{:T(128)}, f32[16,128,256]{2,1,0:T(8,128)S(1)}, s32[16,8]{1,0:T(8,128)S(1)}, bf16[16,128,256]{2,1,0:T(8,128)(2,1)}, bf16[16,128,256]{2,1,0:T(8...) while((s32[]{:T(128)}, f32[16,128,256]{2,1,0:T(8,128)S(1)}, ...), condition=%wide.region_6.7_spmd, body=%wide.region_4.6_spmd.sunk | while | flops 135267360 | bytes 6450065 | solution.py:64
  256.3 1.8 gather_fusion
  262.5 1.8 gather_fusion
  268.7 1.8 gather_fusion
  274.9 1.8 gather_fusion
  281.0 1.8 gather_fusion
  287.2 1.8 gather_fusion
  293.4 1.8 gather_fusion
  299.6 1.8 gather_fusion
  305.8 1.8 gather_fusion
  312.0 1.8 gather_fusion
  318.2 1.8 gather_fusion
  324.4 1.8 gather_fusion
  330.6 1.8 gather_fusion
  335.4 1.3 scatter_fusion
  336.7 1.8 gather_fusion
  343.0 1.8 gather_fusion
  349.2 1.8 gather_fusion
  355.3 3.3 add.105
  358.6 215.7 %reduce-scatter.2.cloned.1.call-done = f32[64,256]{1,0:T(8,128)} async-done(((f32[2048,256]{1,0:T(8,128)}), f32[64,256]{1,0:T(8,128)}) %reduce-scatter.2.cloned.1.call-update) | async-done | bytes 65552 | tf_op jit(solution)/shard_map/reduce_scatter | solution.py:104
  574.4 6.0 %collective-permute-start.1 = (f32[64,256]{1,0:T(8,128)}, f32[64,256]{1,0:T(8,128)S(1)}, u32[]{:S(2)}, u32[]{:S(2)}) collective-permute-start(f32[64,256]{1,0:T(8,128)} %reduce-scatter.2.cloned.1.call-done), channel_id=1, source_target_pairs={{0,32},{32,0},{1,33},{33,1},{2,34},{34,2},{3,35},{35,3},{4,36},{36... | collective-permute-start | bytes 196616 | tf_op jit(solution)/shard_map/ppermute | solution.py:14
  (332 shorter events, 143.8 us)
Async XLA Ops:
  6.5 10.7 %copy-start.4 = (u32[256]{0:T(256)S(1)}, u32[256]{0:T(256)}, u32[]{:S(2)}) copy-start(u32[256]{0:T(256)} %constant.78) | copy-start | bytes 3076
  6.5 12.0 %copy-start.3 = (bf16[64]{0:T(256)(128)(2,1)S(1)}, bf16[64]{0:T(256)(128)(2,1)}, u32[]{:S(2)}) copy-start(bf16[64]{0:T(256)(128)(2,1)} %param.11) | copy-start | bytes 388
  6.5 74.5 %copy-start.2 = (bf16[2,512]{1,0:T(2,128)(2,1)S(1)}, bf16[2,512]{1,0:T(2,128)(2,1)}, u32[]{:S(2)}) copy-start(bf16[2,512]{1,0:T(2,128)(2,1)} %param.13) | copy-start | bytes 6148
  6.5 84.2 %all-gather.6.cloned.1.call-start = ((), (), s32[]{:S(2)}) async-start(), calls=%async_computation.1 | async-start | bytes 2621440 | tf_op jit(solution)/shard_map/all_gather | solution.py:73
  7.3 86.5 %all-gather.8.cloned.1.call-start = ((), (), s32[]{:S(2)}) async-start(), calls=%async_computation.2 | async-start | bytes 2621440 | tf_op jit(solution)/shard_map/all_gather | solution.py:74
  7.3 5.0 collective-permute-start
  12.3 0.8 copy-start.1
  13.2 142.3 %all-gather.10.cloned.1.call-start = ((), (), s32[]{:S(2)}) async-start(), calls=%async_computation.4 | async-start | bytes 1081344 | tf_op jit(solution)/shard_map/all_gather | solution.py:78
  13.9 560.5 %reduce-scatter.2.cloned.1.call-start = ((), (), s32[]{:S(2)}) async-start(), calls=%async_computation.3 | async-start | bytes 2162688 | tf_op jit(solution)/shard_map/reduce_scatter | solution.py:104
  254.7 1.4 copy-start
  574.4 7.1 %collective-permute-start.1 = (f32[64,256]{1,0:T(8,128)}, f32[64,256]{1,0:T(8,128)S(1)}, u32[]{:S(2)}, u32[]{:S(2)}) collective-permute-start(f32[64,256]{1,0:T(8,128)} %reduce-scatter.2.cloned.1.call-done), channel_id=1, source_target_pairs={{0,32},{32,0},{1,33},{33,1},{2,34},{34,2},{3,35},{35,3},{4,36},{36... | collective-permute-start | bytes 196616 | tf_op jit(solution)/shard_map/ppermute | solution.py:14
Sparse Core Ops, SparseCore 0:
  9.1 36.9 all-gather.5
  48.0 33.3 all-gather.7
  84.0 71.4 all-gather.9
  358.8 215.5 reduce-scatter.1
where the time goes:
time: 593 us; the launch traced here: 589 us
  waiting for transfers between devices  279 us (47%)
  local copies, waits for them, and re-layouts  90.2 us (15%)
  matrix products  74.5 us (13%)
  blocking collectives  71 us (12%)
  other arithmetic  48.8 us (8%)
  between operations  13.9 us (2%)
  starting transfers between devices  9.42 us (2%)
    reduce_scatter x1, waiting for transfers between devices, local(): shares = lax.psum_scatter(summed, 'obs', scatter_dimension=0, tiled=True)  216 us
    unnamed x1, blocking collectives  62.3 us
    all_gather x1, waiting for transfers between devices, local(): lax.all_gather(state_own[0], 'obs', axis=0, tiled=True)  58.7 us
    gather x32, local copies, waits for them, and re-layouts, visit(): gathered = state_tiles[blocks_here].reshape(-1, member_count)  57.8 us
    scatter-add x32, other arithmetic, visit(): running.at[blocks_here].add(additions.reshape(-1, edge_size, member_count))  42.6 us
    dot_general x32, matrix products, visit(): lax.dot_general(gathered, obs_tile, (((1,), (1,)), ((), ())), preferred_e...  38.7 us
    dot_general x32, matrix products, visit(): additions = jnp.dot(scaled, weight_tile, preferred_element_type=jnp.float32)  35.8 us
    gather x32, local copies, waits for them, and re-layouts, visit(): positions = place_tiles[blocks_here].reshape(-1)  17.8 us
  transfers between devices with their start and end apart: 6, of which 4 were waited for; matrix products, arithmetic and copies ran while one was open for 2% of the time, Pallas kernels for 0%

commit v1 on v0

--- a/solution.py
+++ b/solution.py
@@ -75,7 +75,10 @@
         lax.all_gather(place_column, "rows", axis=2, tiled=True),
     )
     state_full, place_full = (
-        lax.all_gather(state_own[0], "obs", axis=0, tiled=True),
+        jnp.concatenate(
+            lax.all_to_all(jnp.stack([state_own[0]] * lax.psum(1, "obs"), axis=0), "obs", 0, 0),
+            axis=0,
+        ),
         lax.all_gather(state_pos, "obs", axis=0, tiled=True),
     )
     first_block = lax.axis_index("rows") * ROW_BLOCKS

time: 593 us -> 563 us (0.949)
  waiting for transfers between devices: 279 us -> 232 us
  starting transfers between devices: 9.42 us -> 19 us
  blocking collectives: 71 us -> 77.4 us
    all_gather x1 -> x0, waiting for transfers between devices: 58.7 us -> none  [local(): lax.all_gather(state_own[0], 'obs', axis=0, tiled=True)]
    reduce_scatter x1, waiting for transfers between devices: 216 us -> 230 us  [local(): shares = lax.psum_scatter(summed, 'obs', scatter_dimension=0, tiled=True)]
    all_to_all x0 -> x1, starting transfers between devices: none -> 9.59 us  [local(): lax.all_to_all(jnp.stack([state_own[0]] * lax.psum(1, 'obs'), axis=0), 'o...]
    unnamed x1, blocking collectives: 62.3 us -> 68.3 us
  transfers between devices with their start and end apart: 6 -> 6, of which waited for: 4 -> 2; matrix products, arithmetic and copies ran while one was open for 2% -> 2% of each run, Pallas kernels for 0% -> 0%
where the time goes in v1:
time: 563 us; the launch traced here: 559 us
  waiting for transfers between devices  232 us (41%)
  local copies, waits for them, and re-layouts  91.5 us (16%)
  blocking collectives  77.4 us (14%)
  matrix products  74.5 us (13%)
  other arithmetic  48.8 us (9%)
  starting transfers between devices  19 us (3%)
  between operations  14 us (2%)
    reduce_scatter x1, waiting for transfers between devices, local(): shares = lax.psum_scatter(summed, 'obs', scatter_dimension=0, tiled=True)  230 us
    unnamed x1, blocking collectives  68.3 us
    gather x32, local copies, waits for them, and re-layouts, visit(): gathered = state_tiles[blocks_here].reshape(-1, member_count)  57.8 us
    scatter-add x32, other arithmetic, visit(): running.at[blocks_here].add(additions.reshape(-1, edge_size, member_count))  42.6 us
    dot_general x32, matrix products, visit(): lax.dot_general(gathered, obs_tile, (((1,), (1,)), ((), ())), preferred_e...  38.7 us
    dot_general x32, matrix products, visit(): additions = jnp.dot(scaled, weight_tile, preferred_element_type=jnp.float32)  35.8 us
    gather x32, local copies, waits for them, and re-layouts, visit(): positions = place_tiles[blocks_here].reshape(-1)  17.8 us
  transfers between devices with their start and end apart: 6, of which 2 were waited for; matrix products, arithmetic and copies ran while one was open for 2% of the time, Pallas kernels for 0%

profile of v1, /device:TPU:1, one launch (start us, length us, event | category | flops | bytes accessed | tf_op | source)
XLA Modules:
  0.0 558.9 jit_solution(7591297065108748451)
XLA Ops:
  7.3 3.3 collective-permute-start
  10.6 2.0 stack.3
  12.5 9.6 %all-to-all-start = ((bf16[32,64,256]{2,1,0:T(8,128)(2,1)}), bf16[32,64,256]{2,1,0:T(8,128)(2,1)}, u32[]{:S(2)}, u32[]{:S(2)}) async-start(bf16[32,64,256]{2,1,0:T(8,128)(2,1)} %stack.3), calls=%async_computation | async-start | bytes 2097152 | tf_op jit(solution)/shard_map/all_to_all | solution.py:79
  26.8 68.3 %all-reduce = bf16[2048]{0:T(1024)(128)(2,1)S(1)} all-reduce(bf16[2048]{0:T(1024)(128)(2,1)S(1)} %dynamic-update-slice), channel_id=1, replica_groups=mesh['rows'=4,'half'=2,'obs'=32] {'obs'}, use_global_device_ids=true, to_apply=%add | all-reduce | flops 2048 | bytes 8192
  95.1 9.2 %all-gather = bf16[2,2048]{1,0:T(2,128)(2,1)S(1)} all-gather(bf16[2,512]{1,0:T(2,128)(2,1)S(1)} %copy-done.3), channel_id=2, replica_groups=mesh['rows'=4,'half'=2,'obs'=32] {'rows'}, dimensions={1}, use_global_device_ids=true | all-gather | bytes 10240 | tf_op jit(solution)/shard_map/all_gather | solution.py:75
  105.5 3.0 fusion.36
  108.6 3.0 fusion.35
  111.8 99.0 %while.21 = (s32[]{:T(128)}, f32[16,128,256]{2,1,0:T(8,128)S(1)}, s32[16,8]{1,0:T(8,128)S(1)}, bf16[16,128,256]{2,1,0:T(8,128)(2,1)}, bf16[16,128,256]{2,1,0:T(8...) while((s32[]{:T(128)}, f32[16,128,256]{2,1,0:T(8,128)S(1)}, ...), condition=%wide.region_13.14_spmd, body=%wide.region_11.13_spmd.sunk | while | flops 135267360 | bytes 6450065 | solution.py:64
  111.8 1.8 gather_fusion.2
  116.6 1.3 scatter_fusion.1
  118.0 1.8 gather_fusion.2
  122.8 1.3 scatter_fusion.1
  124.2 1.8 gather_fusion.2
  130.4 1.8 gather_fusion.2
  136.6 1.8 gather_fusion.2
  142.8 1.8 gather_fusion.2
  149.0 1.8 gather_fusion.2
  155.2 1.8 gather_fusion.2
  161.4 1.8 gather_fusion.2
  167.6 1.8 gather_fusion.2
  173.7 1.8 gather_fusion.2
  179.9 1.8 gather_fusion.2
  186.1 1.8 gather_fusion.2
  192.3 1.8 gather_fusion.2
  198.5 1.8 gather_fusion.2
  204.7 1.8 gather_fusion.2
  210.8 1.3 copy-done
  212.4 99.1 %while.20 = (s32[]{:T(128)}, f32[16,128,256]{2,1,0:T(8,128)S(1)}, s32[16,8]{1,0:T(8,128)S(1)}, bf16[16,128,256]{2,1,0:T(8,128)(2,1)}, bf16[16,128,256]{2,1,0:T(8...) while((s32[]{:T(128)}, f32[16,128,256]{2,1,0:T(8,128)S(1)}, ...), condition=%wide.region_6.7_spmd, body=%wide.region_4.6_spmd.sunk | while | flops 135267360 | bytes 6450065 | solution.py:64
  212.4 1.8 gather_fusion
  218.6 1.8 gather_fusion
  224.8 1.8 gather_fusion
  231.0 1.8 gather_fusion
  237.2 1.8 gather_fusion
  243.4 1.8 gather_fusion
  249.6 1.8 gather_fusion
  255.8 1.8 gather_fusion
  262.0 1.8 gather_fusion
  268.2 1.8 gather_fusion
  274.3 1.8 gather_fusion
  280.5 1.8 gather_fusion
  286.7 1.8 gather_fusion
  291.5 1.3 scatter_fusion
  292.9 1.8 gather_fusion
  299.1 1.8 gather_fusion
  305.3 1.8 gather_fusion
  311.5 3.3 add.105
  314.8 229.8 %reduce-scatter.2.cloned.1.call-done = f32[64,256]{1,0:T(8,128)} async-done(((f32[2048,256]{1,0:T(8,128)}), f32[64,256]{1,0:T(8,128)}) %reduce-scatter.2.cloned.1.call-update) | async-done | bytes 65552 | tf_op jit(solution)/shard_map/reduce_scatter | solution.py:107
  544.6 6.0 %collective-permute-start.1 = (f32[64,256]{1,0:T(8,128)}, f32[64,256]{1,0:T(8,128)S(1)}, u32[]{:S(2)}, u32[]{:S(2)}) collective-permute-start(f32[64,256]{1,0:T(8,128)} %reduce-scatter.2.cloned.1.call-done), channel_id=1, source_target_pairs={{0,32},{32,0},{1,33},{33,1},{2,34},{34,2},{3,35},{35,3},{4,36},{36... | collective-permute-start | bytes 196616 | tf_op jit(solution)/shard_map/ppermute | solution.py:14
  (334 shorter events, 142.3 us)
Async XLA Ops:
  6.5 16.7 %copy-start.2 = (s32[2,512,16]{1,2,0:T(8,128)S(1)}, s32[2,512,16]{1,2,0:T(8,128)}, u32[]{:S(2)}) copy-start(s32[2,512,16]{1,2,0:T(8,128)} %param.15) | copy-start | bytes 196612
  6.5 99.0 %all-gather.4.cloned.1.call-start = ((), (), s32[]{:S(2)}) async-start(), calls=%async_computation.2 | async-start | bytes 2621440 | tf_op jit(solution)/shard_map/all_gather | solution.py:73
  7.3 14.9 %collective-permute-start = (bf16[2,1,512,256]{3,2,1,0:T(8,128)(2,1)}, bf16[2,1,512,256]{3,2,1,0:T(8,128)(2,1)S(1)}, u32[]{:S(2)}, u32[]{:S(2)}) collective-permute-start(bf16[2,1,512,256]{3,2,1,0:T(8,128)(2,1)} %param.14), channel_id=1, source_target_pairs={{0,32},{32,0},{1,33},{33,1},{2,34},{34,2},{3,35},{35,3},{4,36},{36... | collective-permute-start | bytes 1572872 | tf_op jit(solution)/shard_map/ppermute | solution.py:14
  10.5 14.7 %copy-start.5 = (u32[256]{0:T(256)S(1)}, u32[256]{0:T(256)}, u32[]{:S(2)}) copy-start(u32[256]{0:T(256)} %constant.78) | copy-start | bytes 3076
  10.5 16.0 %copy-start.4 = (bf16[64]{0:T(256)(128)(2,1)S(1)}, bf16[64]{0:T(256)(128)(2,1)}, u32[]{:S(2)}) copy-start(bf16[64]{0:T(256)(128)(2,1)} %param.11) | copy-start | bytes 388
  12.5 82.5 %copy-start.3 = (bf16[2,512]{1,0:T(2,128)(2,1)S(1)}, bf16[2,512]{1,0:T(2,128)(2,1)}, u32[]{:S(2)}) copy-start(bf16[2,512]{1,0:T(2,128)(2,1)} %param.13) | copy-start | bytes 6148
  12.5 99.1 %all-to-all-start = ((bf16[32,64,256]{2,1,0:T(8,128)(2,1)}), bf16[32,64,256]{2,1,0:T(8,128)(2,1)}, u32[]{:S(2)}, u32[]{:S(2)}) async-start(bf16[32,64,256]{2,1,0:T(8,128)(2,1)} %stack.3), calls=%async_computation | async-start | bytes 2097152 | tf_op jit(solution)/shard_map/all_to_all | solution.py:79
  22.1 86.4 %all-gather.6.cloned.1.call-start = ((), (), s32[]{:S(2)}) async-start(), calls=%async_computation.3 | async-start | bytes 2621440 | tf_op jit(solution)/shard_map/all_gather | solution.py:74
  22.2 0.8 copy-start.1
  23.0 521.6 %reduce-scatter.2.cloned.1.call-start = ((), (), s32[]{:S(2)}) async-start(), calls=%async_computation.4 | async-start | bytes 2162688 | tf_op jit(solution)/shard_map/reduce_scatter | solution.py:107
  210.8 1.4 copy-start
  544.6 7.1 %collective-permute-start.1 = (f32[64,256]{1,0:T(8,128)}, f32[64,256]{1,0:T(8,128)S(1)}, u32[]{:S(2)}, u32[]{:S(2)}) collective-permute-start(f32[64,256]{1,0:T(8,128)} %reduce-scatter.2.cloned.1.call-done), channel_id=1, source_target_pairs={{0,32},{32,0},{1,33},{33,1},{2,34},{34,2},{3,35},{35,3},{4,36},{36... | collective-permute-start | bytes 196616 | tf_op jit(solution)/shard_map/ppermute | solution.py:14
Sparse Core Ops, SparseCore 0:
  9.1 37.0 all-gather.3
  48.0 33.3 all-gather.5
  314.9 229.6 reduce-scatter.1
